TPU v7x, 512 devices: a whole 4x8x8 slice. The times are simulated.
512 devices in a mesh: ctx: 16 (over z, core), tis: 8 (over y), rep: 4 (over x).
Axes of the slice: x: 4, y: 8, z: 8, core: 2. Of those that a mesh axis runs over, the one named last changes fastest.
Arguments:
- donor_feat: bfloat16 [4, 256, 256], P('rep', 'ctx'), may hold values from -6 to 6
- acceptor_feat: bfloat16 [4, 256, 256], P('rep', 'ctx'), may hold values from -6 to 6
- donor_pos: int32 [4, 256], P('rep', 'ctx'), may hold values from 0 to 65535
- acceptor_pos: int32 [4, 256], P('rep'), may hold values from 0 to 65535
- pair_mask: int32 [4, 256, 80], P('rep', 'ctx'), may hold values from 0 to 1
- targets: int32 [4, 256, 32], P('rep', 'ctx', 'tis'), may hold values from 0 to 80, as said below
- dist_table: bfloat16 [128, 256], replicated, may hold values from -3 to 3
- hidden_weights: bfloat16 [32, 256, 512], P('tis'), may hold values from -0.375 to 0.375
- output_weights: bfloat16 [32, 512], P('tis')
Outputs:
- donor_loss: float32 [4, 256, 32], P('rep', 'ctx', 'tis')
- grad_hidden: float32 [32, 256, 512], P('tis', ('ctx', 'rep'))
- grad_acceptor: float32 [4, 256, 256], P('rep', 'ctx')
Inputs may be any that keep to these rules, and one draw needn't show every extreme that they name: `targets`: each target is a valid slot of its donor, or 80 for no splice.
All inputs are finite; a program needn't handle non-finite values.
Results may differ from a plain program's by a relative error of at most 0.002.
The roundings to bfloat16 on the way count: a program that leaves them out, or rounds other values in their place, can miss the bound.
Values may be sent and summed in bfloat16 or wider, within the bound.
A program may use at most 64 MiB of HBM per device.

v0:
```python
import jax
import jax.numpy as jnp
from jax import lax
from jax.sharding import PartitionSpec as P

BLOCK_BP = 65536
SPAN_BLOCKS = 4
BIN_BP = 2048
BINS = 128


def passed_along(value, axis, steps):
    count = lax.axis_size(axis)
    first, last = (max(0, -steps), min(count, count - steps))
    return lax.ppermute(value, axis, [(source, source + steps) for source in range(first, last)])


def silu_grad(values):
    sig = jax.nn.sigmoid(values)
    return sig * (1.0 + values * (1.0 - sig))


def on_device(
    donor_feat,
    acceptor_feat,
    donor_pos,
    acceptor_pos,
    pair_mask,
    targets,
    dist_table,
    hidden_weights,
    output_weights,
):
    seq_dev, don_blk, width = donor_feat.shape
    acc_blk = acceptor_feat.shape[1]
    blocks = lax.axis_size("ctx")
    reach = SPAN_BLOCKS + 1
    slots = reach * acc_blk
    here = lax.axis_index("ctx")
    pieces = [acceptor_feat]
    current = acceptor_feat
    for offset in range(1, reach):
        current = passed_along(current, "ctx", -1)
        pieces.append(current)
    window = jnp.stack(pieces, axis=1).reshape(seq_dev, slots, width)
    pos_pad = jnp.concatenate(
        [acceptor_pos, jnp.zeros((seq_dev, SPAN_BLOCKS * acc_blk), jnp.int32)], axis=1
    )
    pos_win = lax.dynamic_slice_in_dim(pos_pad, here * acc_blk, slots, 1)
    slot_block = jnp.arange(slots, dtype=jnp.int32) // acc_blk
    inchain = here + slot_block < blocks
    dist = slot_block * BLOCK_BP + pos_win[:, None, :] - donor_pos[:, :, None]
    valid = (pair_mask > 0) & (dist > 0) & (dist <= SPAN_BLOCKS * BLOCK_BP) & inchain[None, None, :]
    bins = jnp.clip((dist - 1) // BIN_BP, 0, BINS - 1)
    lookup = (
        (bins[..., None] == jnp.arange(BINS, dtype=jnp.int32))
        .astype(jnp.bfloat16)
        .reshape(-1, BINS)
    )
    table = jnp.dot(lookup, dist_table, preferred_element_type=jnp.float32).reshape(
        seq_dev, don_blk, slots, width
    )
    pre = (
        donor_feat.astype(jnp.float32)[:, :, None, :] + window.astype(jnp.float32)[:, None] + table
    )
    flat = jax.nn.silu(pre).astype(jnp.bfloat16).reshape(-1, width)
    grad_pair = jnp.zeros((flat.shape[0], width), jnp.float32)
    losses = []
    fulls = []
    slot_ids = jnp.arange(slots, dtype=jnp.int32)
    for tissue in range(hidden_weights.shape[0]):
        w_in = hidden_weights[tissue]
        w_out = output_weights[tissue]
        goal = targets[:, :, tissue]
        hid = jnp.dot(flat, w_in, preferred_element_type=jnp.float32)
        act = jax.nn.silu(hid).astype(jnp.bfloat16)
        logits = jnp.dot(act, w_out, preferred_element_type=jnp.float32).reshape(
            seq_dev, don_blk, slots
        )
        masked = jnp.where(valid, logits, -jnp.inf)
        top = jnp.maximum(jnp.max(masked, axis=-1), 0.0)
        expo = jnp.exp(masked - top[..., None])
        total = jnp.sum(expo, axis=-1) + jnp.exp(-top)
        picked = jnp.take_along_axis(logits, jnp.minimum(goal, slots - 1)[..., None], axis=-1)[
            ..., 0
        ]
        picked = jnp.where(goal == slots, 0.0, picked)
        losses.append(top + jnp.log(total) - picked)
        onehot = (goal[..., None] == slot_ids).astype(jnp.float32)
        grad_logits = expo / total[..., None] - onehot
        grad_act = grad_logits.reshape(-1)[:, None] * w_out.astype(jnp.float32)[None, :]
        grad_hid = (grad_act * silu_grad(hid)).astype(jnp.bfloat16)
        grad_pair = grad_pair + lax.dot_general(
            grad_hid, w_in, (((1,), (1,)), ((), ())), preferred_element_type=jnp.float32
        )
        fulls.append(
            lax.dot_general(
                flat, grad_hid, (((0,), (0,)), ((), ())), preferred_element_type=jnp.float32
            )
        )
    stacked = jnp.stack(fulls, axis=1)
    grad_hidden = jnp.transpose(
        lax.psum_scatter(stacked, ("ctx", "rep"), scatter_dimension=0, tiled=True), (1, 0, 2)
    )
    grad_pre = grad_pair.reshape(seq_dev, don_blk, slots, width) * silu_grad(pre)
    contrib = jnp.sum(grad_pre, axis=1).reshape(seq_dev, reach, acc_blk, width)
    carried = contrib[:, reach - 1]
    for offset in range(reach - 2, -1, -1):
        carried = passed_along(carried, "ctx", 1) + contrib[:, offset]
    grad_acceptor = lax.psum(carried, "tis")
    donor_loss = jnp.stack(losses, axis=-1)
    return (donor_loss, grad_hidden, grad_acceptor)


def solution(mesh):
    placed = (
        P("rep", "ctx", None),
        P("rep", "ctx", None),
        P("rep", "ctx"),
        P("rep", None),
        P("rep", "ctx", None),
        P("rep", "ctx", "tis"),
        P(),
        P("tis", None, None),
        P("tis", None),
    )
    return jax.shard_map(
        on_device,
        mesh=mesh,
        in_specs=placed,
        out_specs=(P("rep", "ctx", "tis"), P("tis", ("ctx", "rep"), None), P("rep", "ctx", None)),
        check_vma=False,
    )
```

profile of v0, /device:TPU:8, one launch (start us, length us, event | category | flops | bytes accessed | tf_op | source)
XLA Modules:
  0.0 280.9 jit_solution(4810384354852864490)
XLA Ops:
  7.2 1.3 collective-permute-start
  8.5 0.7 constant_dynamic-update-slice_fusion.4
  9.2 0.7 bitcast_convert_fusion.1
  9.9 0.8 slice_bitcast_fusion.8
  10.8 0.9 slice_reduce_fusion.3
  11.6 0.8 bitcast_add_fusion.4
  12.4 0.7 fusion.28
  13.2 1.3 collective-permute-start.1
  14.6 2.4 collective-permute-done.1
  16.9 1.3 collective-permute-start.2
  18.2 3.9 %collective-permute-done.2 = bf16[1,16,256]{2,1,0:T(8,128)(2,1)S(1)} collective-permute-done((bf16[1,16,256]{2,1,0:T(8,128)(2,1)S(1)}, bf16[1,16,256]{2,1,0:T(8,128)(2,1)S(1)}, u32[]{:S(2)}, u32[]{:S(2)}) %collective-permute-start.2) | collective-permute-done | bytes 8224 | tf_op jit(solution)/shard_map/ppermute | solution.py:15
  22.2 1.3 collective-permute-start.3
  23.5 3.7 %collective-permute-done.3 = bf16[1,16,256]{2,1,0:T(8,128)(2,1)S(1)} collective-permute-done((bf16[1,16,256]{2,1,0:T(8,128)(2,1)S(1)}, bf16[1,16,256]{2,1,0:T(8,128)(2,1)S(1)}, u32[]{:S(2)}, u32[]{:S(2)}) %collective-permute-start.3) | collective-permute-done | bytes 8224 | tf_op jit(solution)/shard_map/ppermute | solution.py:15
  27.2 1.7 multiply_convert_fusion.8
  28.9 0.9 multiply_convert_fusion.7
  29.7 2.3 multiply_convert_fusion.4
  32.0 2.3 multiply_convert_fusion.5
  34.3 2.3 multiply_convert_fusion.6
  37.2 0.6 fusion.42
  37.7 0.6 fusion.44
  38.3 0.6 fusion.46
  39.5 1.0 multiply_convert_fusion.3
  40.5 1.4 convolution_bitcast_fusion.3
  41.9 2.5 fusion.10
  44.5 2.7 multiply_convert_fusion
  47.2 1.3 convolution_bitcast_fusion
  48.6 2.7 multiply_convert_fusion.1
  51.3 1.3 convolution_bitcast_fusion.1
  52.8 2.7 multiply_convert_fusion.2
  56.0 0.8 copy-done.1
  57.1 0.6 convolution_add_fusion.2
  57.7 0.6 convolution_add_fusion.1
  58.9 0.7 copy-done.5
  60.1 4.3 %collective-permute-start.4 = (f32[1,16,256]{2,1,0:T(8,128)S(1)}, f32[1,16,256]{2,1,0:T(8,128)S(1)}, u32[]{:S(2)}, u32[]{:S(2)}) collective-permute-start(f32[1,16,256]{2,1,0:T(8,128)S(1)} %slice_bitcast_fusion.4), channel_id=1, source_target_pairs={{0,32},{32,64},{64,96},{96,128},{128,160},{160,192},{192,224},{224... | collective-permute-start | bytes 49160 | tf_op jit(solution)/shard_map/ppermute | solution.py:15
  64.5 1.5 pad_maximum_fusion
  66.0 2.0 collective-permute-start.5
  68.0 1.3 dynamic-slice
  70.0 0.7 gather_fusion
  70.6 0.7 gather_fusion.1
  71.3 0.7 gather_fusion.3
  72.0 0.7 gather_fusion.2
  72.6 4.3 %collective-permute-start.6 = (f32[1,16,256]{2,1,0:T(8,128)S(1)}, f32[1,16,256]{2,1,0:T(8,128)S(1)}, u32[]{:S(2)}, u32[]{:S(2)}) collective-permute-start(f32[1,16,256]{2,1,0:T(8,128)S(1)} %fusion.25), channel_id=1, source_target_pairs={{0,32},{32,64},{64,96},{96,128},{128,160},{160,192},{192,224},{224... | collective-permute-start | bytes 49160 | tf_op jit(solution)/shard_map/ppermute | solution.py:15
  77.0 0.8 collective-permute-done.6
  77.8 2.2 collective-permute-start.7
  80.0 0.6 pad_maximum_fusion.1
  80.8 30.4 %psum.7 = f32[1,16,256]{2,1,0:T(8,128)} all-reduce(f32[1,16,256]{2,1,0:T(8,128)S(1)} %fusion.23), channel_id=1, replica_groups=mesh['ctx'=16,'tis'=8,'rep'=4] {'tis'}, use_global_device_ids=true, to_apply=%region_10.12 | all-reduce | flops 4096 | bytes 32768 | tf_op jit(solution)/shard_map/psum | solution.py:110
  111.2 161.4 %all-reduce.4.cloned.1.call-done = f32[256,4,512]{2,0,1:T(8,128)} async-done(((f32[256,4,512]{2,0,1:T(8,128)}), f32[256,4,512]{2,0,1:T(8,128)}) %all-reduce.4.cloned.1.call-update) | async-done | bytes 2097168
  272.6 1.5 dynamic-slice_bitcast_fusion
  (65 shorter events, 3.7 us)
Async XLA Ops:
  7.2 20.0 %copy-start = (bf16[128,256]{1,0:T(8,128)(2,1)S(1)}, bf16[128,256]{1,0:T(8,128)(2,1)}, u32[]{:S(2)}) copy-start(bf16[128,256]{1,0:T(8,128)(2,1)} %param.17) | copy-start | bytes 196612
  7.2 265.4 %all-reduce.4.cloned.1.call-start = ((), (), s32[]{:S(2)}) async-start(), calls=%async_computation | async-start | bytes 4194304
  7.2 6.0 %collective-permute-start = (bf16[1,16,256]{2,1,0:T(8,128)(2,1)}, bf16[1,16,256]{2,1,0:T(8,128)(2,1)S(1)}, u32[]{:S(2)}, u32[]{:S(2)}) collective-permute-start(bf16[1,16,256]{2,1,0:T(8,128)(2,1)} %param.12), channel_id=1, source_target_pairs={{32,0},{64,32},{96,64},{128,96},{160,128},{192,160},{224,192},{256... | collective-permute-start | bytes 24584 | tf_op jit(solution)/shard_map/ppermute | solution.py:15
  13.2 3.7 %collective-permute-start.1 = (bf16[1,16,256]{2,1,0:T(8,128)(2,1)S(1)}, bf16[1,16,256]{2,1,0:T(8,128)(2,1)S(1)}, u32[]{:S(2)}, u32[]{:S(2)}) collective-permute-start(bf16[1,16,256]{2,1,0:T(8,128)(2,1)S(1)} %collective-permute-done), channel_id=1, source_target_pairs={{32,0},{64,32},{96,64},{128,96},{160,128},{192,160},{224,192},{256... | collective-permute-start | bytes 24584 | tf_op jit(solution)/shard_map/ppermute | solution.py:15
  16.9 5.2 %collective-permute-start.2 = (bf16[1,16,256]{2,1,0:T(8,128)(2,1)S(1)}, bf16[1,16,256]{2,1,0:T(8,128)(2,1)S(1)}, u32[]{:S(2)}, u32[]{:S(2)}) collective-permute-start(bf16[1,16,256]{2,1,0:T(8,128)(2,1)S(1)} %collective-permute-done.1), channel_id=1, source_target_pairs={{32,0},{64,32},{96,64},{128,96},{160,128},{192,160},{224,192},{256... | collective-permute-start | bytes 24584 | tf_op jit(solution)/shard_map/ppermute | solution.py:15
  22.2 5.0 %collective-permute-start.3 = (bf16[1,16,256]{2,1,0:T(8,128)(2,1)S(1)}, bf16[1,16,256]{2,1,0:T(8,128)(2,1)S(1)}, u32[]{:S(2)}, u32[]{:S(2)}) collective-permute-start(bf16[1,16,256]{2,1,0:T(8,128)(2,1)S(1)} %collective-permute-done.2), channel_id=1, source_target_pairs={{32,0},{64,32},{96,64},{128,96},{160,128},{192,160},{224,192},{256... | collective-permute-start | bytes 24584 | tf_op jit(solution)/shard_map/ppermute | solution.py:15
  27.1 1.7 copy-start.6
  34.3 2.3 copy-start.8
  37.1 1.7 copy-start.10
  37.2 1.7 copy-start.11
  55.5 1.3 copy-start.1
  55.5 1.6 copy-start.7
  58.3 1.3 copy-start.5
  58.9 5.6 %copy-start.2 = (f32[256,1,512]{2,0,1:T(8,128)S(1)}, f32[256,1,512]{2,0,1:T(8,128)}, u32[]{:S(2)}) copy-start(f32[256,1,512]{2,0,1:T(8,128)} %convolution_bitcast_fusion.3) | copy-start | bytes 1572868
  58.9 5.6 %copy-start.3 = (f32[256,1,512]{2,0,1:T(8,128)S(1)}, f32[256,1,512]{2,0,1:T(8,128)}, u32[]{:S(2)}) copy-start(f32[256,1,512]{2,0,1:T(8,128)} %convolution_bitcast_fusion) | copy-start | bytes 1572868
  58.9 5.6 %copy-start.4 = (f32[256,1,512]{2,0,1:T(8,128)S(1)}, f32[256,1,512]{2,0,1:T(8,128)}, u32[]{:S(2)}) copy-start(f32[256,1,512]{2,0,1:T(8,128)} %convolution_bitcast_fusion.1) | copy-start | bytes 1572868
  60.1 5.8 %collective-permute-start.4 = (f32[1,16,256]{2,1,0:T(8,128)S(1)}, f32[1,16,256]{2,1,0:T(8,128)S(1)}, u32[]{:S(2)}, u32[]{:S(2)}) collective-permute-start(f32[1,16,256]{2,1,0:T(8,128)S(1)} %slice_bitcast_fusion.4), channel_id=1, source_target_pairs={{0,32},{32,64},{64,96},{96,128},{128,160},{160,192},{192,224},{224... | collective-permute-start | bytes 49160 | tf_op jit(solution)/shard_map/ppermute | solution.py:15
  66.0 11.0 %copy-start.9 = (s32[1,16,4]{1,2,0:T(4,128)S(1)}, s32[1,16,4]{1,2,0:T(4,128)}, u32[]{:S(2)}) copy-start(s32[1,16,4]{1,2,0:T(4,128)} %param.16) | copy-start | bytes 772
  66.0 6.6 %collective-permute-start.5 = (f32[1,16,256]{2,1,0:T(8,128)S(1)}, f32[1,16,256]{2,1,0:T(8,128)S(1)}, u32[]{:S(2)}, u32[]{:S(2)}) collective-permute-start(f32[1,16,256]{2,1,0:T(8,128)S(1)} %fusion.26), channel_id=1, source_target_pairs={{0,32},{32,64},{64,96},{96,128},{128,160},{160,192},{192,224},{224... | collective-permute-start | bytes 49160 | tf_op jit(solution)/shard_map/ppermute | solution.py:15
  72.6 5.1 %collective-permute-start.6 = (f32[1,16,256]{2,1,0:T(8,128)S(1)}, f32[1,16,256]{2,1,0:T(8,128)S(1)}, u32[]{:S(2)}, u32[]{:S(2)}) collective-permute-start(f32[1,16,256]{2,1,0:T(8,128)S(1)} %fusion.25), channel_id=1, source_target_pairs={{0,32},{32,64},{64,96},{96,128},{128,160},{160,192},{192,224},{224... | collective-permute-start | bytes 49160 | tf_op jit(solution)/shard_map/ppermute | solution.py:15
  77.8 3.1 %collective-permute-start.7 = (f32[1,16,256]{2,1,0:T(8,128)S(1)}, f32[1,16,256]{2,1,0:T(8,128)S(1)}, u32[]{:S(2)}, u32[]{:S(2)}) collective-permute-start(f32[1,16,256]{2,1,0:T(8,128)S(1)} %fusion.24), channel_id=1, source_target_pairs={{0,32},{32,64},{64,96},{96,128},{128,160},{160,192},{192,224},{224... | collective-permute-start | bytes 49160 | tf_op jit(solution)/shard_map/ppermute | solution.py:15
Sparse Core Ops, SparseCore 0:
  66.1 206.4 all-reduce.3
where the time goes:
time: 282 us; the launch traced here: 281 us
  waiting for transfers between devices  172 us (61%)
  blocking collectives  30.4 us (11%)
  matrix products  20.5 us (7%)
  starting transfers between devices  18 us (6%)
  other arithmetic  15.4 us (5%)
  between operations  15.1 us (5%)
  local copies, waits for them, and re-layouts  9.11 us (3%)
    unnamed x2, waiting for transfers between devices  161 us
    psum x1, blocking collectives, on_device(): grad_acceptor = lax.psum(carried, 'tis')  30.4 us
    ppermute x8, starting transfers between devices, passed_along(): lax.ppermute(value, axis, [(source, source + steps) for source in range(f...  18 us
    ppermute x8, waiting for transfers between devices, passed_along(): lax.ppermute(value, axis, [(source, source + steps) for source in range(f...  11 us
    convert_element_type x4, other arithmetic, on_device(): grad_hid = (grad_act * silu_grad(hid)).astype(jnp.bfloat16)  9.15 us
    dot_general x4, matrix products, on_device(): hid = jnp.dot(flat, w_in, preferred_element_type=jnp.float32)  7.74 us
  transfers between devices with their start and end apart: 9, of which 6 were waited for; matrix products, arithmetic and copies ran while one was open for 4% of the time, Pallas kernels for 0%

commit v1 on v0

--- a/solution.py
+++ b/solution.py
@@ -107,7 +107,10 @@
     carried = contrib[:, reach - 1]
     for offset in range(reach - 2, -1, -1):
         carried = passed_along(carried, "ctx", 1) + contrib[:, offset]
-    grad_acceptor = lax.psum(carried, "tis")
+    devices, grad_acceptor = (lax.axis_size("tis"), carried)
+    for far in [1 << k for k in range(devices.bit_length() - 1)]:
+        route = [(i, i ^ far) for i in range(devices)]
+        grad_acceptor = grad_acceptor + lax.ppermute(grad_acceptor, "tis", route)
     donor_loss = jnp.stack(losses, axis=-1)
     return (donor_loss, grad_hidden, grad_acceptor)
 

time: 282 us -> 292 us (1.035)
  blocking collectives: 30.4 us -> 0 us
  waiting for transfers between devices: 172 us -> 199 us
  starting transfers between devices: 18 us -> 32.1 us
    psum x1 -> x0, blocking collectives: 30.4 us -> none  [on_device(): grad_acceptor = lax.psum(carried, 'tis')]
    unnamed x2, waiting for transfers between devices: 161 us -> 177 us
    ppermute x0 -> x3, starting transfers between devices: none -> 12 us  [on_device(): grad_acceptor = grad_acceptor + lax.ppermute(grad_acceptor, 'tis', route)]
    ppermute x0 -> x3, waiting for transfers between devices: none -> 10.8 us  [on_device(): grad_acceptor = grad_acceptor + lax.ppermute(grad_acceptor, 'tis', route)]
  transfers between devices with their start and end apart: 9 -> 12, of which waited for: 6 -> 9; matrix products, arithmetic and copies ran while one was open for 4% -> 4% of each run, Pallas kernels for 0% -> 0%
where the time goes in v1:
time: 292 us; the launch traced here: 291 us
  waiting for transfers between devices  199 us (68%)
  starting transfers between devices  32.1 us (11%)
  matrix products  18.9 us (6%)
  other arithmetic  16.1 us (6%)
  between operations  15.1 us (5%)
  local copies, waits for them, and re-layouts  9.26 us (3%)
    unnamed x2, waiting for transfers between devices  177 us
    ppermute x8, starting transfers between devices, passed_along(): lax.ppermute(value, axis, [(source, source + steps) for source in range(f...  20.1 us
    ppermute x3, starting transfers between devices, on_device(): grad_acceptor = grad_acceptor + lax.ppermute(grad_acceptor, 'tis', route)  12 us
    ppermute x8, waiting for transfers between devices, passed_along(): lax.ppermute(value, axis, [(source, source + steps) for source in range(f...  11.4 us
    ppermute x3, waiting for transfers between devices, on_device(): grad_acceptor = grad_acceptor + lax.ppermute(grad_acceptor, 'tis', route)  10.8 us
    convert_element_type x4, other arithmetic, on_device(): grad_hid = (grad_act * silu_grad(hid)).astype(jnp.bfloat16)  9.24 us
    dot_general x4, matrix products, on_device(): hid = jnp.dot(flat, w_in, preferred_element_type=jnp.float32)  9.22 us
  transfers between devices with their start and end apart: 12, of which 9 were waited for; matrix products, arithmetic and copies ran while one was open for 4% of the time, Pallas kernels for 0%

profile of v1, /device:TPU:8, one launch (start us, length us, event | category | flops | bytes accessed | tf_op | source)
XLA Modules:
  0.0 291.0 jit_solution(11426984809509607333)
XLA Ops:
  7.2 1.3 collective-permute-start
  8.5 0.7 constant_dynamic-update-slice_fusion.4
  9.2 0.7 bitcast_convert_fusion.1
  9.9 0.8 slice_bitcast_fusion.8
  10.8 0.9 slice_reduce_fusion.3
  11.6 0.8 bitcast_add_fusion.4
  12.4 0.7 fusion.28
  13.2 1.3 collective-permute-start.1
  14.5 2.4 collective-permute-done.1
  16.9 1.3 collective-permute-start.2
  18.2 3.9 %collective-permute-done.2 = bf16[1,16,256]{2,1,0:T(8,128)(2,1)S(1)} collective-permute-done((bf16[1,16,256]{2,1,0:T(8,128)(2,1)S(1)}, bf16[1,16,256]{2,1,0:T(8,128)(2,1)S(1)}, u32[]{:S(2)}, u32[]{:S(2)}) %collective-permute-start.2) | collective-permute-done | bytes 8224 | tf_op jit(solution)/shard_map/ppermute | solution.py:15
  22.1 1.3 collective-permute-start.3
  23.4 3.7 %collective-permute-done.3 = bf16[1,16,256]{2,1,0:T(8,128)(2,1)S(1)} collective-permute-done((bf16[1,16,256]{2,1,0:T(8,128)(2,1)S(1)}, bf16[1,16,256]{2,1,0:T(8,128)(2,1)S(1)}, u32[]{:S(2)}, u32[]{:S(2)}) %collective-permute-start.3) | collective-permute-done | bytes 8224 | tf_op jit(solution)/shard_map/ppermute | solution.py:15
  27.1 1.6 multiply_convert_fusion.8
  28.8 2.3 multiply_convert_fusion.7
  31.0 2.4 multiply_convert_fusion.4
  33.4 2.3 multiply_convert_fusion.5
  35.7 2.3 multiply_convert_fusion.6
  38.5 0.6 fusion.42
  39.1 0.6 fusion.44
  40.9 2.7 multiply_convert_fusion
  43.6 1.3 convolution_bitcast_fusion
  45.1 2.7 multiply_convert_fusion.1
  47.8 1.4 convolution_bitcast_fusion.1
  49.3 2.8 multiply_convert_fusion.3
  52.7 1.2 copy-done.1
  53.9 1.0 multiply_convert_fusion.2
  56.5 0.8 copy-done.4
  57.8 4.4 %collective-permute-start.4 = (f32[1,16,256]{2,1,0:T(8,128)S(1)}, f32[1,16,256]{2,1,0:T(8,128)S(1)}, u32[]{:S(2)}, u32[]{:S(2)}) collective-permute-start(f32[1,16,256]{2,1,0:T(8,128)S(1)} %slice_bitcast_fusion.4), channel_id=1, source_target_pairs={{0,32},{32,64},{64,96},{96,128},{128,160},{160,192},{192,224},{224... | collective-permute-start | bytes 49160 | tf_op jit(solution)/shard_map/ppermute | solution.py:15
  63.1 2.2 collective-permute-start.5
  66.1 4.1 %collective-permute-start.6 = (f32[1,16,256]{2,1,0:T(8,128)S(1)}, f32[1,16,256]{2,1,0:T(8,128)S(1)}, u32[]{:S(2)}, u32[]{:S(2)}) collective-permute-start(f32[1,16,256]{2,1,0:T(8,128)S(1)} %fusion.25), channel_id=1, source_target_pairs={{0,32},{32,64},{64,96},{96,128},{128,160},{160,192},{192,224},{224... | collective-permute-start | bytes 49160 | tf_op jit(solution)/shard_map/ppermute | solution.py:15
  70.2 1.5 pad_maximum_fusion
  71.7 4.2 %collective-permute-start.7 = (f32[1,16,256]{2,1,0:T(8,128)S(1)}, f32[1,16,256]{2,1,0:T(8,128)S(1)}, u32[]{:S(2)}, u32[]{:S(2)}) collective-permute-start(f32[1,16,256]{2,1,0:T(8,128)S(1)} %fusion.24), channel_id=1, source_target_pairs={{0,32},{32,64},{64,96},{96,128},{128,160},{160,192},{192,224},{224... | collective-permute-start | bytes 49160 | tf_op jit(solution)/shard_map/ppermute | solution.py:15
  76.0 0.8 collective-permute-done.7
  76.8 7.3 %collective-permute-start.8 = (f32[1,16,256]{2,1,0:T(8,128)S(1)}, f32[1,16,256]{2,1,0:T(8,128)S(1)}, u32[]{:S(2)}, u32[]{:S(2)}) collective-permute-start(f32[1,16,256]{2,1,0:T(8,128)S(1)} %fusion.23), channel_id=1, source_target_pairs={{0,4},{4,0},{8,12},{12,8},{16,20},{20,16},{24,28},{28,24},{1,5},{5... | collective-permute-start | bytes 49160 | tf_op jit(solution)/shard_map/ppermute | solution.py:113
  84.1 1.3 dynamic-slice
  86.1 0.7 gather_fusion
  86.7 0.7 gather_fusion.1
  87.4 0.7 gather_fusion.3
  88.0 0.7 gather_fusion.2
  88.7 1.9 collective-permute-start.9
  90.7 4.6 %collective-permute-done.9 = f32[1,16,256]{2,1,0:T(8,128)S(1)} collective-permute-done((f32[1,16,256]{2,1,0:T(8,128)S(1)}, f32[1,16,256]{2,1,0:T(8,128)S(1)}, u32[]{:S(2)}, u32[]{:S(2)}) %collective-permute-start.9) | collective-permute-done | bytes 16416 | tf_op jit(solution)/shard_map/ppermute | solution.py:113
  95.3 2.7 collective-permute-start.10
  98.0 0.6 pad_maximum_fusion.1
  98.6 6.2 %collective-permute-done.10 = f32[1,16,256]{2,1,0:T(8,128)S(1)} collective-permute-done((f32[1,16,256]{2,1,0:T(8,128)S(1)}, f32[1,16,256]{2,1,0:T(8,128)S(1)}, u32[]{:S(2)}, u32[]{:S(2)}) %collective-permute-start.10) | collective-permute-done | bytes 16416 | tf_op jit(solution)/shard_map/ppermute | solution.py:113
  104.8 0.6 add.302
  105.4 177.3 %all-reduce.4.cloned.1.call-done = f32[256,4,512]{2,0,1:T(8,128)} async-done(((f32[256,4,512]{2,0,1:T(8,128)}), f32[256,4,512]{2,0,1:T(8,128)}) %all-reduce.4.cloned.1.call-update) | async-done | bytes 2097168
  282.6 1.5 dynamic-slice_bitcast_fusion
  (71 shorter events, 6.5 us)
Async XLA Ops:
  7.2 20.0 %copy-start = (bf16[128,256]{1,0:T(8,128)(2,1)S(1)}, bf16[128,256]{1,0:T(8,128)(2,1)}, u32[]{:S(2)}) copy-start(bf16[128,256]{1,0:T(8,128)(2,1)} %param.17) | copy-start | bytes 196612
  7.2 275.5 %all-reduce.4.cloned.1.call-start = ((), (), s32[]{:S(2)}) async-start(), calls=%async_computation | async-start | bytes 4194304
  7.2 6.0 %collective-permute-start = (bf16[1,16,256]{2,1,0:T(8,128)(2,1)}, bf16[1,16,256]{2,1,0:T(8,128)(2,1)S(1)}, u32[]{:S(2)}, u32[]{:S(2)}) collective-permute-start(bf16[1,16,256]{2,1,0:T(8,128)(2,1)} %param.12), channel_id=1, source_target_pairs={{32,0},{64,32},{96,64},{128,96},{160,128},{192,160},{224,192},{256... | collective-permute-start | bytes 24584 | tf_op jit(solution)/shard_map/ppermute | solution.py:15
  13.2 3.7 %collective-permute-start.1 = (bf16[1,16,256]{2,1,0:T(8,128)(2,1)S(1)}, bf16[1,16,256]{2,1,0:T(8,128)(2,1)S(1)}, u32[]{:S(2)}, u32[]{:S(2)}) collective-permute-start(bf16[1,16,256]{2,1,0:T(8,128)(2,1)S(1)} %collective-permute-done), channel_id=1, source_target_pairs={{32,0},{64,32},{96,64},{128,96},{160,128},{192,160},{224,192},{256... | collective-permute-start | bytes 24584 | tf_op jit(solution)/shard_map/ppermute | solution.py:15
  16.9 5.2 %collective-permute-start.2 = (bf16[1,16,256]{2,1,0:T(8,128)(2,1)S(1)}, bf16[1,16,256]{2,1,0:T(8,128)(2,1)S(1)}, u32[]{:S(2)}, u32[]{:S(2)}) collective-permute-start(bf16[1,16,256]{2,1,0:T(8,128)(2,1)S(1)} %collective-permute-done.1), channel_id=1, source_target_pairs={{32,0},{64,32},{96,64},{128,96},{160,128},{192,160},{224,192},{256... | collective-permute-start | bytes 24584 | tf_op jit(solution)/shard_map/ppermute | solution.py:15
  22.1 5.0 %collective-permute-start.3 = (bf16[1,16,256]{2,1,0:T(8,128)(2,1)S(1)}, bf16[1,16,256]{2,1,0:T(8,128)(2,1)S(1)}, u32[]{:S(2)}, u32[]{:S(2)}) collective-permute-start(bf16[1,16,256]{2,1,0:T(8,128)(2,1)S(1)} %collective-permute-done.2), channel_id=1, source_target_pairs={{32,0},{64,32},{96,64},{128,96},{160,128},{192,160},{224,192},{256... | collective-permute-start | bytes 24584 | tf_op jit(solution)/shard_map/ppermute | solution.py:15
  27.1 1.6 copy-start.5
  35.7 2.3 copy-start.7
  38.5 1.7 copy-start.9
  38.5 1.7 copy-start.10
  49.3 2.8 copy-start.6
  52.1 1.7 copy-start.1
  55.9 1.3 copy-start.4
  57.7 12.4 %copy-start.2 = (f32[256,1,512]{2,0,1:T(8,128)S(1)}, f32[256,1,512]{2,0,1:T(8,128)}, u32[]{:S(2)}) copy-start(f32[256,1,512]{2,0,1:T(8,128)} %convolution_bitcast_fusion) | copy-start | bytes 1572868
  57.8 12.4 %copy-start.3 = (f32[256,1,512]{2,0,1:T(8,128)S(1)}, f32[256,1,512]{2,0,1:T(8,128)}, u32[]{:S(2)}) copy-start(f32[256,1,512]{2,0,1:T(8,128)} %convolution_bitcast_fusion.1) | copy-start | bytes 1572868
  57.8 5.3 %collective-permute-start.4 = (f32[1,16,256]{2,1,0:T(8,128)S(1)}, f32[1,16,256]{2,1,0:T(8,128)S(1)}, u32[]{:S(2)}, u32[]{:S(2)}) collective-permute-start(f32[1,16,256]{2,1,0:T(8,128)S(1)} %slice_bitcast_fusion.4), channel_id=1, source_target_pairs={{0,32},{32,64},{64,96},{96,128},{128,160},{160,192},{192,224},{224... | collective-permute-start | bytes 49160 | tf_op jit(solution)/shard_map/ppermute | solution.py:15
  63.1 3.1 %collective-permute-start.5 = (f32[1,16,256]{2,1,0:T(8,128)S(1)}, f32[1,16,256]{2,1,0:T(8,128)S(1)}, u32[]{:S(2)}, u32[]{:S(2)}) collective-permute-start(f32[1,16,256]{2,1,0:T(8,128)S(1)} %fusion.26), channel_id=1, source_target_pairs={{0,32},{32,64},{64,96},{96,128},{128,160},{160,192},{192,224},{224... | collective-permute-start | bytes 49160 | tf_op jit(solution)/shard_map/ppermute | solution.py:15
  66.1 5.6 %collective-permute-start.6 = (f32[1,16,256]{2,1,0:T(8,128)S(1)}, f32[1,16,256]{2,1,0:T(8,128)S(1)}, u32[]{:S(2)}, u32[]{:S(2)}) collective-permute-start(f32[1,16,256]{2,1,0:T(8,128)S(1)} %fusion.25), channel_id=1, source_target_pairs={{0,32},{32,64},{64,96},{96,128},{128,160},{160,192},{192,224},{224... | collective-permute-start | bytes 49160 | tf_op jit(solution)/shard_map/ppermute | solution.py:15
  71.7 19.0 %copy-start.8 = (s32[1,16,4]{1,2,0:T(4,128)S(1)}, s32[1,16,4]{1,2,0:T(4,128)}, u32[]{:S(2)}) copy-start(s32[1,16,4]{1,2,0:T(4,128)} %param.16) | copy-start | bytes 772
  71.7 5.0 %collective-permute-start.7 = (f32[1,16,256]{2,1,0:T(8,128)S(1)}, f32[1,16,256]{2,1,0:T(8,128)S(1)}, u32[]{:S(2)}, u32[]{:S(2)}) collective-permute-start(f32[1,16,256]{2,1,0:T(8,128)S(1)} %fusion.24), channel_id=1, source_target_pairs={{0,32},{32,64},{64,96},{96,128},{128,160},{160,192},{192,224},{224... | collective-permute-start | bytes 49160 | tf_op jit(solution)/shard_map/ppermute | solution.py:15
  76.8 11.9 %collective-permute-start.8 = (f32[1,16,256]{2,1,0:T(8,128)S(1)}, f32[1,16,256]{2,1,0:T(8,128)S(1)}, u32[]{:S(2)}, u32[]{:S(2)}) collective-permute-start(f32[1,16,256]{2,1,0:T(8,128)S(1)} %fusion.23), channel_id=1, source_target_pairs={{0,4},{4,0},{8,12},{12,8},{16,20},{20,16},{24,28},{28,24},{1,5},{5... | collective-permute-start | bytes 49160 | tf_op jit(solution)/shard_map/ppermute | solution.py:113
  88.7 6.5 %collective-permute-start.9 = (f32[1,16,256]{2,1,0:T(8,128)S(1)}, f32[1,16,256]{2,1,0:T(8,128)S(1)}, u32[]{:S(2)}, u32[]{:S(2)}) collective-permute-start(f32[1,16,256]{2,1,0:T(8,128)S(1)} %add.300), channel_id=1, source_target_pairs={{0,8},{4,12},{8,0},{12,4},{16,24},{20,28},{24,16},{28,20},{1,9},{5... | collective-permute-start | bytes 49160 | tf_op jit(solution)/shard_map/ppermute | solution.py:113
  95.3 9.5 %collective-permute-start.10 = (f32[1,16,256]{2,1,0:T(8,128)S(1)}, f32[1,16,256]{2,1,0:T(8,128)S(1)}, u32[]{:S(2)}, u32[]{:S(2)}) collective-permute-start(f32[1,16,256]{2,1,0:T(8,128)S(1)} %add.301), channel_id=1, source_target_pairs={{0,16},{4,20},{8,24},{12,28},{16,0},{20,4},{24,8},{28,12},{1,17},{... | collective-permute-start | bytes 49160 | tf_op jit(solution)/shard_map/ppermute | solution.py:113
Sparse Core Ops, SparseCore 0:
  71.8 210.7 all-reduce.3
